TPU v7x, 32 devices: a whole 2x2x4 slice. The times are simulated.
32 devices in a mesh: dp: 8 (over z, x), tp: 4 (over y, core).
Axes of the slice: x: 2, y: 2, z: 4, core: 2. Of those that a mesh axis runs over, the one named last changes fastest.
Arguments:
- inputs: bfloat16 [2, 4096, 768], P(None, 'dp'), may hold values from -6 to 6
- cotangent: bfloat16 [2, 4096, 768], P(None, 'dp'), may hold values from -6 to 6
- item_ids: int32 [2, 4096], P(None, 'dp'), may hold values from 0 to 3584, as said below
- timestep: int32 [2, 8], P(None, 'dp'), may hold values from 0 to 999
- qkv_weight: float32 [768, 3, 768], P('dp', None, 'tp'), may hold values from -0.21875 to 0.21875
- out_weight: float32 [768, 768], P('tp', 'dp'), may hold values from -0.625 to 0.625
- up_weight: float32 [768, 3072], P('dp', 'tp'), may hold values from -0.21875 to 0.21875
- down_weight: float32 [3072, 768], P('tp', 'dp'), may hold values from -0.109375 to 0.109375
- norm_params: float32 [4, 768], P(None, 'dp')
- qkv_first: float32 [768, 3, 768], P('dp', None, 'tp'), may hold values from -0.00061035156 to 0.00061035156
- out_first: float32 [768, 768], P('tp', 'dp'), may hold values from -0.00061035156 to 0.00061035156
- up_first: float32 [768, 3072], P('dp', 'tp'), may hold values from -0.00061035156 to 0.00061035156
- down_first: float32 [3072, 768], P('tp', 'dp'), may hold values from -0.00061035156 to 0.00061035156
- norm_first: float32 [4, 768], P(None, 'dp'), may hold values from -0.001953125 to 0.001953125
- qkv_second: float32 [768, 3, 768], P('dp', None, 'tp'), may hold values from 1.4122378e-10 to 5.6489513e-10
- out_second: float32 [768, 768], P('tp', 'dp'), may hold values from 1.4122378e-10 to 5.6489513e-10
- up_second: float32 [768, 3072], P('dp', 'tp'), may hold values from 1.4122378e-10 to 5.6489513e-10
- down_second: float32 [3072, 768], P('tp', 'dp'), may hold values from 1.4122378e-10 to 5.6489513e-10
- norm_second: float32 [4, 768], P(None, 'dp'), may hold values from 1.4122379e-09 to 5.6489515e-09
Outputs:
- block_out: bfloat16 [2, 4096, 768], P(None, 'dp')
- input_grad: float32 [2, 4096, 768], P(None, 'dp')
- grad_norm: float32 [], replicated
- qkv_new: float32 [768, 3, 768], P('dp', None, 'tp')
- qkv_first_new: float32 [768, 3, 768], P('dp', None, 'tp')
- qkv_second_new: float32 [768, 3, 768], P('dp', None, 'tp')
- out_new: float32 [768, 768], P('tp', 'dp')
- out_first_new: float32 [768, 768], P('tp', 'dp')
- out_second_new: float32 [768, 768], P('tp', 'dp')
- up_new: float32 [768, 3072], P('dp', 'tp')
- up_first_new: float32 [768, 3072], P('dp', 'tp')
- up_second_new: float32 [768, 3072], P('dp', 'tp')
- down_new: float32 [3072, 768], P('tp', 'dp')
- down_first_new: float32 [3072, 768], P('tp', 'dp')
- down_second_new: float32 [3072, 768], P('tp', 'dp')
- norm_new: float32 [4, 768], P(None, 'dp')
- norm_first_new: float32 [4, 768], P(None, 'dp')
- norm_second_new: float32 [4, 768], P(None, 'dp')
Inputs may be any that keep to these rules, and one draw needn't show every extreme that they name: `item_ids`: A token's id is the index, within its micro-batch, of its item's first token, so ids never decrease along a micro-batch; every block of 512 tokens of one index of dp starts a new item, so no item spans two blocks; an item has 1 to 512 tokens and in every draw some item has exactly 512.
All inputs are finite; a program needn't handle non-finite values.
Results may differ from a plain program's by a relative error of at most 0.009.
Values may be sent and summed in bfloat16 or wider, within the bound.
A program may use at most 128 MiB of HBM per device.

v0:
```python
from functools import partial
import math
import jax
import jax.numpy as jnp
from jax import lax
from jax.sharding import PartitionSpec as P

HEAD_DIM = 64
STEP = 10
norm_eps = 1e-05
clip_limit = 1.0
learn_rate = 0.02
beta_one = 0.9
beta_two = 0.999
adam_eps = 1e-08
weight_decay = 0.01


def time_embed(step_values, model_width):
    half_width = model_width // 2
    frequency = jnp.exp(
        jnp.arange(half_width, dtype=jnp.float32) * (-math.log(10000.0) / half_width)
    )
    angles = step_values.astype(jnp.float32)[..., None] * frequency
    return jnp.concatenate([jnp.sin(angles), jnp.cos(angles)], axis=-1)


def layer_norm(values, gain_row, bias_row):
    centre = values - jnp.mean(values, axis=-1, keepdims=True)
    spread = jnp.mean(centre * centre, axis=-1, keepdims=True)
    return centre * lax.rsqrt(spread + norm_eps) * gain_row + bias_row


def masked_scores(query_rows, key_rows, same_item, score_scale):
    scores = (
        jnp.einsum("thd,shd->hts", query_rows, key_rows, preferred_element_type=jnp.float32)
        * score_scale
    )
    return jnp.where(same_item, scores, -1e30)


def one_micro(gathered, stream_in, upstream, labels, embed_row):
    qkv_mat, out_mat, up_mat, down_mat, norm_rows = gathered
    tokens_here = stream_in.shape[0]
    local_width = out_mat.shape[0]
    heads_here = local_width // HEAD_DIM
    score_scale = 1.0 / math.sqrt(HEAD_DIM)
    split_shape = (tokens_here, heads_here, HEAD_DIM)
    norm_gains = norm_rows.astype(jnp.float32)
    gain_one = 1.0 + norm_gains[0]
    gain_two = 1.0 + norm_gains[2]
    stream = stream_in.astype(jnp.float32) + embed_row[None, :]
    normed_f, norm_one_back = jax.vjp(layer_norm, stream, gain_one, norm_gains[1])
    normed = normed_f.astype(jnp.bfloat16)
    triple = jnp.einsum("td,dje->jte", normed, qkv_mat, preferred_element_type=jnp.float32).astype(
        jnp.bfloat16
    )
    query_rows = triple[0].reshape(split_shape)
    key_rows = triple[1].reshape(split_shape)
    value_rows = triple[2].reshape(split_shape)
    same_item = (labels[:, None] == labels[None, :])[None]
    scores = masked_scores(query_rows, key_rows, same_item, score_scale)
    row_top = jnp.max(scores, axis=-1, keepdims=True)
    exp_scores = jnp.exp(scores - row_top)
    row_total = jnp.sum(exp_scores, axis=-1, keepdims=True)
    probs_soft = exp_scores / row_total
    log_total = row_top + jnp.log(row_total)
    context = (
        jnp.einsum(
            "hts,shd->thd",
            probs_soft.astype(jnp.bfloat16),
            value_rows,
            preferred_element_type=jnp.float32,
        )
        .reshape(tokens_here, local_width)
        .astype(jnp.bfloat16)
    )
    attn_out = lax.psum(jnp.dot(context, out_mat, preferred_element_type=jnp.float32), "tp")
    middle = stream + attn_out
    normed_two_f, norm_two_back = jax.vjp(layer_norm, middle, gain_two, norm_gains[3])
    normed_two = normed_two_f.astype(jnp.bfloat16)
    hidden_pre = jnp.dot(normed_two, up_mat, preferred_element_type=jnp.float32)
    hidden_f, gelu_back = jax.vjp(partial(jax.nn.gelu, approximate=False), hidden_pre)
    hidden = hidden_f.astype(jnp.bfloat16)
    branch = lax.psum(
        jnp.dot(hidden, down_mat, preferred_element_type=jnp.float32).astype(jnp.bfloat16), "tp"
    ).astype(jnp.float32)
    block_out = (middle + branch).astype(jnp.bfloat16)
    grad_down = jnp.einsum("tf,td->fd", hidden, upstream, preferred_element_type=jnp.float32)
    grad_hidden = jnp.einsum("td,fd->tf", upstream, down_mat, preferred_element_type=jnp.float32)
    grad_pre = gelu_back(grad_hidden)[0].astype(jnp.bfloat16)
    grad_up = jnp.einsum("td,tf->df", normed_two, grad_pre, preferred_element_type=jnp.float32)
    grad_normed_two = lax.psum(
        jnp.einsum("tf,df->td", grad_pre, up_mat, preferred_element_type=jnp.float32), "tp"
    )
    grad_middle_norm, grad_gain_two, grad_bias_two = norm_two_back(grad_normed_two)
    grad_middle = upstream.astype(jnp.float32) + grad_middle_norm
    grad_attn = grad_middle.astype(jnp.bfloat16)
    grad_outmat = jnp.einsum("tc,td->cd", context, grad_attn, preferred_element_type=jnp.float32)
    grad_context = (
        jnp.einsum("td,cd->tc", grad_attn, out_mat, preferred_element_type=jnp.float32)
        .astype(jnp.bfloat16)
        .reshape(split_shape)
    )
    probs_again = jnp.exp(masked_scores(query_rows, key_rows, same_item, score_scale) - log_total)
    grad_values = jnp.einsum(
        "hts,thd->shd",
        probs_again.astype(jnp.bfloat16),
        grad_context,
        preferred_element_type=jnp.float32,
    )
    grad_probs = jnp.einsum(
        "thd,shd->hts", grad_context, value_rows, preferred_element_type=jnp.float32
    )
    inner_sum = jnp.sum(grad_probs * probs_again, axis=-1, keepdims=True)
    grad_scores = (probs_again * (grad_probs - inner_sum)).astype(jnp.bfloat16)
    grad_query = (
        jnp.einsum("hts,shd->thd", grad_scores, key_rows, preferred_element_type=jnp.float32)
        * score_scale
    )
    grad_key = (
        jnp.einsum("hts,thd->shd", grad_scores, query_rows, preferred_element_type=jnp.float32)
        * score_scale
    )
    grad_triple = (
        jnp.stack([grad_query, grad_key, grad_values])
        .reshape(3, tokens_here, local_width)
        .astype(jnp.bfloat16)
    )
    grad_qkv = jnp.einsum("td,jte->dje", normed, grad_triple, preferred_element_type=jnp.float32)
    grad_normed = lax.psum(
        jnp.einsum("jte,dje->td", grad_triple, qkv_mat, preferred_element_type=jnp.float32).astype(
            jnp.bfloat16
        ),
        "tp",
    ).astype(jnp.float32)
    grad_stream_norm, grad_gain_one, grad_bias_one = norm_one_back(grad_normed)
    grad_input = grad_middle + grad_stream_norm
    grad_norms = jnp.stack([grad_gain_one, grad_bias_one, grad_gain_two, grad_bias_two])
    return (block_out, grad_input, (grad_qkv, grad_outmat, grad_up, grad_down, grad_norms))


def adam_step(weight, gradient, first_old, second_old):
    first_new = beta_one * first_old + (1.0 - beta_one) * gradient
    second_new = beta_two * second_old + (1.0 - beta_two) * gradient * gradient
    moment_one = first_new / (1.0 - beta_one**STEP)
    moment_two = second_new / (1.0 - beta_two**STEP)
    weight_new = weight - learn_rate * (
        moment_one / (jnp.sqrt(moment_two) + adam_eps) + weight_decay * weight
    )
    return (weight_new, first_new, second_new)


def local(
    inputs,
    cotangent,
    item_ids,
    timestep,
    qkv_weight,
    out_weight,
    up_weight,
    down_weight,
    norm_params,
    qkv_first,
    out_first,
    up_first,
    down_first,
    norm_first,
    qkv_second,
    out_second,
    up_second,
    down_second,
    norm_second,
):
    micro_count = inputs.shape[0]
    embeds = time_embed(timestep[:, 0], inputs.shape[2])
    qkv_low = qkv_weight.astype(jnp.bfloat16)
    out_low = out_weight.astype(jnp.bfloat16)
    up_low = up_weight.astype(jnp.bfloat16)
    down_low = down_weight.astype(jnp.bfloat16)
    norm_low = norm_params.astype(jnp.bfloat16)
    block_list = []
    input_list = []
    for number in range(micro_count):
        gathered = (
            lax.all_gather(qkv_low, "dp", axis=0, tiled=True),
            lax.all_gather(out_low, "dp", axis=1, tiled=True),
            lax.all_gather(up_low, "dp", axis=0, tiled=True),
            lax.all_gather(down_low, "dp", axis=1, tiled=True),
            lax.all_gather(norm_low, "dp", axis=1, tiled=True),
        )
        block_out, grad_input, grad_list = one_micro(
            gathered, inputs[number], cotangent[number], item_ids[number], embeds[number]
        )
        owned_grads = (
            lax.psum_scatter(grad_list[0], "dp", scatter_dimension=0, tiled=True),
            lax.psum_scatter(grad_list[1], "dp", scatter_dimension=1, tiled=True),
            lax.psum_scatter(grad_list[2], "dp", scatter_dimension=0, tiled=True),
            lax.psum_scatter(grad_list[3], "dp", scatter_dimension=1, tiled=True),
            lax.psum_scatter(grad_list[4], "dp", scatter_dimension=1, tiled=True),
        )
        if number == 0:
            totals = tuple(owned_grads)
        else:
            totals = tuple((left + right for left, right in zip(totals, owned_grads)))
        block_list.append(block_out)
        input_list.append(grad_input)
    own_squares = jnp.sum(totals[0] * totals[0]) + jnp.sum(totals[1] * totals[1])
    own_squares = own_squares + jnp.sum(totals[2] * totals[2]) + jnp.sum(totals[3] * totals[3])
    norm_squares = jnp.sum(totals[4] * totals[4])
    own_squares = own_squares + jnp.where(
        lax.axis_index("tp") == 0, norm_squares, jnp.zeros_like(norm_squares)
    )
    grad_norm = jnp.sqrt(lax.psum(own_squares, ("dp", "tp")))
    factor = jnp.minimum(1.0, clip_limit / (grad_norm + 1e-06))
    weights = (qkv_weight, out_weight, up_weight, down_weight, norm_params)
    firsts = (qkv_first, out_first, up_first, down_first, norm_first)
    seconds = (qkv_second, out_second, up_second, down_second, norm_second)
    result = [
        adam_step(weights[index], totals[index] * factor, firsts[index], seconds[index])
        for index in range(5)
    ]
    return (
        jnp.stack(block_list),
        jnp.stack(input_list),
        grad_norm,
        result[0][0],
        result[0][1],
        result[0][2],
        result[1][0],
        result[1][1],
        result[1][2],
        result[2][0],
        result[2][1],
        result[2][2],
        result[3][0],
        result[3][1],
        result[3][2],
        result[4][0],
        result[4][1],
        result[4][2],
    )


def solution(mesh):
    return jax.shard_map(
        local,
        mesh=mesh,
        in_specs=(
            P(None, "dp", None),
            P(None, "dp", None),
            P(None, "dp"),
            P(None, "dp"),
            P("dp", None, "tp"),
            P("tp", "dp"),
            P("dp", "tp"),
            P("tp", "dp"),
            P(None, "dp"),
            P("dp", None, "tp"),
            P("tp", "dp"),
            P("dp", "tp"),
            P("tp", "dp"),
            P(None, "dp"),
            P("dp", None, "tp"),
            P("tp", "dp"),
            P("dp", "tp"),
            P("tp", "dp"),
            P(None, "dp"),
        ),
        out_specs=(
            P(None, "dp", None),
            P(None, "dp", None),
            P(),
            P("dp", None, "tp"),
            P("dp", None, "tp"),
            P("dp", None, "tp"),
            P("tp", "dp"),
            P("tp", "dp"),
            P("tp", "dp"),
            P("dp", "tp"),
            P("dp", "tp"),
            P("dp", "tp"),
            P("tp", "dp"),
            P("tp", "dp"),
            P("tp", "dp"),
            P(None, "dp"),
            P(None, "dp"),
            P(None, "dp"),
        ),
        check_vma=False,
    )
```

profile of v0, /device:TPU:0, one launch (start us, length us, event | category | flops | bytes accessed | tf_op | source)
XLA Modules:
  0.0 723.9 jit_solution(8021237277195858394)
XLA Ops:
  12.2 22.2 %all-gather = bf16[8,96,4]{1,2,0:T(4,128)(2,1)S(1)} all-gather(bf16[1,96,4]{1,2,0:T(4,128)(2,1)S(1)} %convert_bitcast_fusion.2), channel_id=1, replica_groups=mesh['dp'=8,'tp'=4] {'dp'}, dimensions={0}, use_global_device_ids=true | all-gather | bytes 6912 | tf_op jit(solution)/shard_map/all_gather | solution.py:190
  35.3 35.3 %all_gather.21 = bf16[768,3,192]{2,1,0:T(4,128)(2,1)S(1)} all-gather(bf16[96,3,192]{2,1,0:T(4,128)(2,1)S(1)} %copy.82), channel_id=1, replica_groups=mesh['dp'=8,'tp'=4] {'dp'}, dimensions={0}, use_global_device_ids=true | all-gather | bytes 995328 | tf_op jit(solution)/shard_map/all_gather | solution.py:186
  70.6 2.1 copy.83
  72.6 2.0 fusion.107
  77.2 31.1 %all_gather.22 = bf16[192,768]{0,1:T(8,128)(2,1)S(1)} all-gather(bf16[192,96]{0,1:T(8,128)(2,1)S(1)} %copy.85), channel_id=1, replica_groups=mesh['dp'=8,'tp'=4] {'dp'}, dimensions={1}, use_global_device_ids=true | all-gather | bytes 331776 | tf_op jit(solution)/shard_map/all_gather | solution.py:187
  108.3 2.0 fusion.110
  124.4 64.3 %all-reduce.9.cloned.1.call-done = (f32[512,768]{1,0:T(8,128)}, f32[512,768]{1,0:T(8,128)}) async-done(((f32[512,768]{1,0:T(8,128)}, f32[512,768]{1,0:T(8,128)}), (f32[512,768]{1,0:T(8,128)}, f32[512,768]{1,0:T(8,128)})) %all-reduce.9.cloned.1.call-update) | async-done | bytes 3145744 | tf_op jit(solution)/shard_map/psum | solution.py:78
  188.7 3.0 fusion.123
  194.6 7.6 %multiply_convert_fusion.3 = (bf16[512,768]{1,0:T(8,128)(2,1)}, f32[512,768]{1,0:T(8,128)}, f32[512,768]{1,0:T(8,128)}) fusion(bf16[768,768]{1,0:T(8,128)(2,1)} %all-gather.4.cloned.1.call-done, f32[512,768]{1,0:T(8,128)} %copy-done.8, f32[768]{0:T(1024)} %get-tuple-element.39, f32[768]{0:T(1024)} %get-tuple-element.38, f32[512]{0:T(512)} %fusion.99, ...), kind=kOutput, calls=%fused_computation.98 | convolution fusion | flops 631504896 | bytes 6694912 | tf_op jit(solution)/shard_map/dot_general | solution.py:82
  202.2 4.3 all-gather.6.cloned.1.call-done
  206.5 3.6 add_convert_fusion.1
  211.0 2.0 fusion.135
  213.1 5.0 multiply_convert_fusion.2
  220.1 2.0 fusion.136
  224.3 3.4 convolution_convert_fusion.1
  229.5 59.9 %all-reduce.7.cloned.1.call-done = (f32[512,768]{1,0:T(8,128)}, f32[512,768]{1,0:T(8,128)}) async-done(((f32[512,768]{1,0:T(8,128)}, f32[512,768]{1,0:T(8,128)}), (f32[512,768]{1,0:T(8,128)}, f32[512,768]{1,0:T(8,128)})) %all-reduce.7.cloned.1.call-update) | async-done | bytes 3145744 | tf_op jit(solution)/shard_map/psum | solution.py:93
  289.4 4.7 multiply_reduce_fusion.3
  312.8 3.5 fusion.112
  319.4 61.3 %all-reduce.11.cloned.1.call-done = (bf16[512,768]{1,0:T(8,128)(2,1)}, bf16[512,768]{1,0:T(8,128)(2,1)}, bf16[512,768]{1,0:T(8,128)(2,1)}, bf16[512,768]{1,0:T(8,128)(2,1)}) async-done(((bf16[512,768]{1,0:T(8,128)(2,1)}, bf16[512,768]{1,0:T(8,128)(2,1)}, bf16[512,768]{1,0:T(8,128)(2,1)}, bf16[512,768]{1,0:T(8,128)(2,1)}), (bf16[512,768]{1,0:T(8,128)(2,1)}, bf16[512,768]{1,0:T(8,128)(2,1)}, ...) | async-done | bytes 3145744 | tf_op jit(solution)/shard_map/psum | solution.py:85
  380.8 2.5 fusion.9
  383.5 2.5 fusion.12
  387.2 4.4 convolution_add_fusion.1
  391.7 2.3 fusion.78
  394.1 2.3 convolution_add_fusion
  397.3 2.1 fusion.71
  399.5 2.5 convolution_add_fusion.2
  403.8 2.8 add_bitcast_fusion.1
  411.7 37.1 %reduce-scatter.18.cloned.1.call-done = f32[96,4]{1,0:T(8,128)} async-done(((f32[768,4]{1,0:T(8,128)}), f32[96,4]{1,0:T(8,128)}) %reduce-scatter.18.cloned.1.call-update) | async-done | bytes 1552
  450.9 70.0 %reduce-scatter.12.cloned.1.call-done = f32[96,768]{1,0:T(8,128)} async-done(((f32[768,768]{1,0:T(8,128)}), f32[96,768]{1,0:T(8,128)}) %reduce-scatter.12.cloned.1.call-update) | async-done | bytes 294928 | tf_op jit(solution)/shard_map/reduce_scatter | solution.py:198
  522.6 70.3 %reduce-scatter.14.cloned.1.call-done = f32[768,96]{0,1:T(8,128)} async-done(((f32[768,768]{0,1:T(8,128)}), f32[768,96]{0,1:T(8,128)}) %reduce-scatter.14.cloned.1.call-update) | async-done | bytes 294928 | tf_op jit(solution)/shard_map/reduce_scatter | solution.py:199
  594.6 70.2 %reduce-scatter.10.cloned.1.call-done = f32[96,3,192]{2,0,1:T(8,128)} async-done(((f32[768,3,192]{2,0,1:T(8,128)}), f32[96,3,192]{2,0,1:T(8,128)}) %reduce-scatter.10.cloned.1.call-update) | async-done | bytes 221200 | tf_op jit(solution)/shard_map/reduce_scatter | solution.py:196
  670.4 39.6 %psum.71 = f32[]{:T(128)} all-reduce(f32[]{:T(128)S(6)} %add.323), channel_id=1, replica_groups=mesh['dp'=8,'tp'=4] {'dp','tp'}, use_global_device_ids=true, to_apply=%region_53.54 | all-reduce | flops 1 | bytes 8 | tf_op jit(solution)/shard_map/psum | solution.py:214
  (409 shorter events, 73.3 us)
Async XLA Ops:
  8.0 180.7 %all-reduce.9.cloned.1.call-start = ((), (), s32[]{:S(2)}) async-start(), calls=%async_computation.13 | async-start | bytes 6291456 | tf_op jit(solution)/shard_map/psum | solution.py:78
  10.8 61.8 %copy-start.85 = (f32[512]{0:T(512)}, f32[512]{0:T(512)S(1)}, u32[]{:S(2)}) copy-start(f32[512]{0:T(512)S(1)} %get-tuple-element.109) | copy-start | bytes 6148
  10.9 97.4 %copy-start.83 = (f32[512]{0:T(512)}, f32[512]{0:T(512)S(1)}, u32[]{:S(2)}) copy-start(f32[512]{0:T(512)S(1)} %get-tuple-element.108) | copy-start | bytes 6148
  12.1 60.5 %copy-start.104 = (f32[512]{0:T(512)}, f32[512]{0:T(512)S(1)}, u32[]{:S(2)}) copy-start(f32[512]{0:T(512)S(1)} %fusion.98) | copy-start | bytes 6148
  35.1 73.2 %copy-start.75 = (f32[768]{0:T(1024)}, f32[768]{0:T(1024)S(1)}, u32[]{:S(2)}) copy-start(f32[768]{0:T(1024)S(1)} %get-tuple-element.41) | copy-start | bytes 9220
  120.4 74.2 %all-gather.4.cloned.1.call-start = ((), (), s32[]{:S(2)}) async-start(), calls=%async_computation.5 | async-start | bytes 1327104 | tf_op jit(solution)/shard_map/all_gather | solution.py:188
  122.1 84.4 %all-gather.6.cloned.1.call-start = ((), (), s32[]{:S(2)}) async-start(), calls=%async_computation.6 | async-start | bytes 1327104 | tf_op jit(solution)/shard_map/all_gather | solution.py:189
  123.8 165.6 %all-reduce.7.cloned.1.call-start = ((), (), s32[]{:S(2)}) async-start(), calls=%async_computation.12 | async-start | bytes 6291456 | tf_op jit(solution)/shard_map/psum | solution.py:93
  222.1 158.7 %all-reduce.11.cloned.1.call-start = ((), (), s32[]{:S(2)}) async-start(), calls=%async_computation.14 | async-start | bytes 6291456 | tf_op jit(solution)/shard_map/psum | solution.py:85
  311.5 90.5 %reduce-scatter.16.cloned.1.call-start = ((), (), s32[]{:S(2)}) async-start(), calls=%async_computation.10 | async-start | bytes 884736
  318.1 62.6 %copy-start.3 = (bf16[2,512,768]{2,1,0:T(8,128)(2,1)S(1)}, bf16[2,512,768]{2,1,0:T(8,128)(2,1)}, u32[]{:S(2)}) copy-start(bf16[2,512,768]{2,1,0:T(8,128)(2,1)} %param.19) | copy-start | bytes 4718596
  318.1 62.6 %copy-start.76 = (f32[768]{0:T(1024)S(1)}, f32[768]{0:T(1024)}, u32[]{:S(2)}) copy-start(f32[768]{0:T(1024)} %copy-done.75) | copy-start | bytes 9220
  318.2 62.6 %copy-start.84 = (f32[512]{0:T(512)S(1)}, f32[512]{0:T(512)}, u32[]{:S(2)}) copy-start(f32[512]{0:T(512)} %copy-done.83) | copy-start | bytes 6148
  318.2 62.6 %copy-start.86 = (f32[512]{0:T(512)S(1)}, f32[512]{0:T(512)}, u32[]{:S(2)}) copy-start(f32[512]{0:T(512)} %copy-done.85) | copy-start | bytes 6148
  319.4 129.4 %reduce-scatter.18.cloned.1.call-start = ((), (), s32[]{:S(2)}) async-start(), calls=%async_computation.11 | async-start | bytes 442368
  387.1 133.9 %reduce-scatter.12.cloned.1.call-start = ((), (), s32[]{:S(2)}) async-start(), calls=%async_computation.8 | async-start | bytes 2654208 | tf_op jit(solution)/shard_map/reduce_scatter | solution.py:198
  391.6 201.4 %reduce-scatter.14.cloned.1.call-start = ((), (), s32[]{:S(2)}) async-start(), calls=%async_computation.9 | async-start | bytes 2654208 | tf_op jit(solution)/shard_map/reduce_scatter | solution.py:199
  396.3 268.4 %reduce-scatter.10.cloned.1.call-start = ((), (), s32[]{:S(2)}) async-start(), calls=%async_computation.7 | async-start | bytes 2654208 | tf_op jit(solution)/shard_map/reduce_scatter | solution.py:196
  669.0 41.7 %copy-start.135 = (f32[4,96]{1,0:T(4,128)S(1)}, f32[4,96]{1,0:T(4,128)}, u32[]{:S(2)}) copy-start(f32[4,96]{1,0:T(4,128)} %param.27) | copy-start | bytes 4612
  669.0 41.7 %copy-start.139 = (f32[4,96]{1,0:T(4,128)S(1)}, f32[4,96]{1,0:T(4,128)}, u32[]{:S(2)}) copy-start(f32[4,96]{1,0:T(4,128)} %param.32) | copy-start | bytes 4612
  669.0 41.7 %copy-start.140 = (f32[4,96]{1,0:T(4,128)S(1)}, f32[4,96]{1,0:T(4,128)}, u32[]{:S(2)}) copy-start(f32[4,96]{1,0:T(4,128)} %param.37) | copy-start | bytes 4612
  669.0 42.3 %copy-start.59 = (f32[192,96]{1,0:T(8,128)S(1)}, f32[192,96]{1,0:T(8,128)}, u32[]{:S(2)}) copy-start(f32[192,96]{1,0:T(8,128)} %param.24) | copy-start | bytes 221188
  669.0 42.3 %copy-start.77 = (f32[192,96]{1,0:T(8,128)S(1)}, f32[192,96]{1,0:T(8,128)}, u32[]{:S(2)}) copy-start(f32[192,96]{1,0:T(8,128)} %param.29) | copy-start | bytes 221188
  669.1 42.3 %copy-start.78 = (f32[192,96]{1,0:T(8,128)S(1)}, f32[192,96]{1,0:T(8,128)}, u32[]{:S(2)}) copy-start(f32[192,96]{1,0:T(8,128)} %param.34) | copy-start | bytes 221188
  669.1 43.0 %copy-start.36 = (f32[768,96]{0,1:T(8,128)S(1)}, f32[768,96]{0,1:T(8,128)}, u32[]{:S(2)}) copy-start(f32[768,96]{0,1:T(8,128)} %param.26) | copy-start | bytes 884740
  669.1 43.0 %copy-start.41 = (f32[768,96]{0,1:T(8,128)S(1)}, f32[768,96]{0,1:T(8,128)}, u32[]{:S(2)}) copy-start(f32[768,96]{0,1:T(8,128)} %reduce-scatter.14.cloned.1.call-done) | copy-start | bytes 884740
  669.1 43.0 %copy-start.60 = (f32[768,96]{0,1:T(8,128)S(1)}, f32[768,96]{0,1:T(8,128)}, u32[]{:S(2)}) copy-start(f32[768,96]{0,1:T(8,128)} %param.31) | copy-start | bytes 884740
  669.1 43.0 %copy-start.61 = (f32[768,96]{0,1:T(8,128)S(1)}, f32[768,96]{0,1:T(8,128)}, u32[]{:S(2)}) copy-start(f32[768,96]{0,1:T(8,128)} %param.36) | copy-start | bytes 884740
  670.4 42.8 %copy-start.37 = (f32[96,768]{1,0:T(8,128)S(1)}, f32[96,768]{1,0:T(8,128)}, u32[]{:S(2)}) copy-start(f32[96,768]{1,0:T(8,128)} %param.25) | copy-start | bytes 884740
  670.4 42.8 %copy-start.40 = (f32[96,768]{1,0:T(8,128)S(1)}, f32[96,768]{1,0:T(8,128)}, u32[]{:S(2)}) copy-start(f32[96,768]{1,0:T(8,128)} %reduce-scatter.12.cloned.1.call-done) | copy-start | bytes 884740
  670.4 42.8 %copy-start.62 = (f32[96,768]{1,0:T(8,128)S(1)}, f32[96,768]{1,0:T(8,128)}, u32[]{:S(2)}) copy-start(f32[96,768]{1,0:T(8,128)} %param.30) | copy-start | bytes 884740
  670.4 42.8 %copy-start.63 = (f32[96,768]{1,0:T(8,128)S(1)}, f32[96,768]{1,0:T(8,128)}, u32[]{:S(2)}) copy-start(f32[96,768]{1,0:T(8,128)} %param.35) | copy-start | bytes 884740
  (123 other events, 504.9 us)
Sparse Core Ops, SparseCore 0:
  120.5 68.1 all-reduce.8
  222.2 67.1 all-reduce.6
  311.6 69.1 all-reduce.10
Sparse Core Ops, SparseCore 1:
  123.6 40.9 all-gather.3
  166.6 39.9 all-gather.5
  319.5 62.4 reduce-scatter.15
  387.2 61.6 reduce-scatter.17
  452.7 68.2 reduce-scatter.11
  524.9 68.0 reduce-scatter.13
  596.7 68.0 reduce-scatter.9
where the time goes:
time: 731 us; the launch traced here: 724 us
  waiting for transfers between devices  438 us (60%)
  blocking collectives  128 us (18%)
  matrix products  63.2 us (9%)
  other arithmetic  47.9 us (7%)
  local copies, waits for them, and re-layouts  22.8 us (3%)
  between operations  22.4 us (3%)
    reduce_scatter x1, waiting for transfers between devices, local(): lax.psum_scatter(grad_list[3], 'dp', scatter_dimension=1, tiled=True)  70.3 us
    reduce_scatter x1, waiting for transfers between devices, local(): lax.psum_scatter(grad_list[0], 'dp', scatter_dimension=0, tiled=True)  70.2 us
    reduce_scatter x1, waiting for transfers between devices, local(): lax.psum_scatter(grad_list[2], 'dp', scatter_dimension=0, tiled=True)  70 us
    psum x1, waiting for transfers between devices, one_micro(): lax.psum(jnp.dot(context, out_mat, preferred_element_type=jnp.float32), '...  64.3 us
    psum x1, waiting for transfers between devices, one_micro(): lax.psum(jnp.dot(hidden, down_mat, preferred_element_type=jnp.float32).as...  61.3 us
    psum x1, waiting for transfers between devices, one_micro(): lax.psum(jnp.einsum('tf,df->td', grad_pre, up_mat, preferred_element_type...  59.9 us
    psum x1, blocking collectives, local(): grad_norm = jnp.sqrt(lax.psum(own_squares, ('dp', 'tp')))  39.6 us
    unnamed x12, waiting for transfers between devices  37.3 us
  transfers between devices with their start and end apart: 10, of which 8 were waited for; matrix products, arithmetic and copies ran while one was open for 8% of the time, Pallas kernels for 0%

commit v1 on v0

--- a/solution.py
+++ b/solution.py
@@ -4,6 +4,7 @@
 import jax.numpy as jnp
 from jax import lax
 from jax.sharding import PartitionSpec as P
+from jax.lax import all_gather
 
 HEAD_DIM = 64
 STEP = 10
@@ -75,7 +76,8 @@
         .reshape(tokens_here, local_width)
         .astype(jnp.bfloat16)
     )
-    attn_out = lax.psum(jnp.dot(context, out_mat, preferred_element_type=jnp.float32), "tp")
+    block_here = jnp.dot(context, out_mat, preferred_element_type=jnp.float32)
+    attn_out = jnp.sum(all_gather(block_here, "tp"), 0)
     middle = stream + attn_out
     normed_two_f, norm_two_back = jax.vjp(layer_norm, middle, gain_two, norm_gains[3])
     normed_two = normed_two_f.astype(jnp.bfloat16)

time: 731 us -> 880 us (1.20)
  waiting for transfers between devices: 438 us -> 575 us
  other arithmetic: 47.9 us -> 58.3 us
    all_gather x0 -> x2, waiting for transfers between devices: none -> 76.5 us  [one_micro(): attn_out = jnp.sum(all_gather(block_here, 'tp'), 0)]
    psum x1 -> x0, waiting for transfers between devices: 64.3 us -> none  [one_micro(): lax.psum(jnp.dot(context, out_mat, preferred_element_type=jnp.float32), '...]
    unnamed x12 -> x13, waiting for transfers between devices: 37.3 us -> 99.3 us
    all_gather x1, waiting for transfers between devices: 0.01 us -> 33.6 us  [local(): lax.all_gather(up_low, 'dp', axis=0, tiled=True)]
    all_gather x1, waiting for transfers between devices: 4.33 us -> 34.3 us  [local(): lax.all_gather(down_low, 'dp', axis=1, tiled=True)]
    reduce_sum x0 -> x2, other arithmetic: none -> 9.04 us  [one_micro(): attn_out = jnp.sum(all_gather(block_here, 'tp'), 0)]
    unnamed x295 -> x285, local copies, waits for them, and re-layouts: 19.1 us -> 19.9 us
  transfers between devices with their start and end apart: 10 -> 11, of which waited for: 8 -> 11; matrix products, arithmetic and copies ran while one was open for 8% -> 9% of each run, Pallas kernels for 0% -> 0%
where the time goes in v1:
time: 880 us; the launch traced here: 872 us
  waiting for transfers between devices  575 us (65%)
  blocking collectives  128 us (15%)
  matrix products  64.6 us (7%)
  other arithmetic  58.3 us (7%)
  local copies, waits for them, and re-layouts  23.7 us (3%)
  between operations  20.9 us (2%)
    unnamed x13, waiting for transfers between devices  99.3 us
    all_gather x2, waiting for transfers between devices, one_micro(): attn_out = jnp.sum(all_gather(block_here, 'tp'), 0)  76.5 us
    reduce_scatter x1, waiting for transfers between devices, local(): lax.psum_scatter(grad_list[0], 'dp', scatter_dimension=0, tiled=True)  70.2 us
    reduce_scatter x1, waiting for transfers between devices, local(): lax.psum_scatter(grad_list[3], 'dp', scatter_dimension=1, tiled=True)  70.1 us
    reduce_scatter x1, waiting for transfers between devices, local(): lax.psum_scatter(grad_list[2], 'dp', scatter_dimension=0, tiled=True)  69.8 us
    psum x1, waiting for transfers between devices, one_micro(): lax.psum(jnp.dot(hidden, down_mat, preferred_element_type=jnp.float32).as...  61.1 us
    psum x1, waiting for transfers between devices, one_micro(): lax.psum(jnp.einsum('tf,df->td', grad_pre, up_mat, preferred_element_type...  60.2 us
    psum x1, blocking collectives, local(): grad_norm = jnp.sqrt(lax.psum(own_squares, ('dp', 'tp')))  39.5 us
  transfers between devices with their start and end apart: 11, of which 11 were waited for; matrix products, arithmetic and copies ran while one was open for 9% of the time, Pallas kernels for 0%

profile of v1, /device:TPU:0, one launch (start us, length us, event | category | flops | bytes accessed | tf_op | source)
XLA Modules:
  0.0 872.0 jit_solution(12331755158194118148)
XLA Ops:
  11.2 22.2 %all-gather.2 = bf16[8,96,4]{1,2,0:T(4,128)(2,1)S(1)} all-gather(bf16[1,96,4]{1,2,0:T(4,128)(2,1)S(1)} %convert_bitcast_fusion.2), channel_id=1, replica_groups=mesh['dp'=8,'tp'=4] {'dp'}, dimensions={0}, use_global_device_ids=true | all-gather | bytes 6912 | tf_op jit(solution)/shard_map/all_gather | solution.py:192
  34.3 35.3 %all_gather.33 = bf16[768,3,192]{2,1,0:T(4,128)(2,1)S(1)} all-gather(bf16[96,3,192]{2,1,0:T(4,128)(2,1)S(1)} %copy.82), channel_id=1, replica_groups=mesh['dp'=8,'tp'=4] {'dp'}, dimensions={0}, use_global_device_ids=true | all-gather | bytes 995328 | tf_op jit(solution)/shard_map/all_gather | solution.py:188
  76.3 31.1 %all_gather.34 = bf16[192,768]{0,1:T(8,128)(2,1)S(1)} all-gather(bf16[192,96]{0,1:T(8,128)(2,1)S(1)} %copy.85), channel_id=1, replica_groups=mesh['dp'=8,'tp'=4] {'dp'}, dimensions={1}, use_global_device_ids=true | all-gather | bytes 331776 | tf_op jit(solution)/shard_map/all_gather | solution.py:189
  115.0 2.3 fusion.107
  126.8 32.5 %all-gather.14.cloned.1.call-done = f32[2048,768]{1,0:T(8,128)} async-done(((f32[512,768]{1,0:T(8,128)}), f32[2048,768]{1,0:T(8,128)}) %all-gather.14.cloned.1.call-update) | async-done | bytes 6291472 | tf_op jit(solution)/shard_map/all_gather | solution.py:80
  159.3 4.5 reduce_sum.322
  163.8 44.0 %all-gather.12.cloned.1.call-done = f32[2048,768]{1,0:T(8,128)} async-done(((f32[512,768]{1,0:T(8,128)}), f32[2048,768]{1,0:T(8,128)}) %all-gather.12.cloned.1.call-update) | async-done | bytes 6291472 | tf_op jit(solution)/shard_map/all_gather | solution.py:80
  207.8 4.5 reduce_sum.310
  212.4 2.9 fusion.123
  218.1 33.6 %all-gather.8.cloned.1.call-done = bf16[768,768]{1,0:T(8,128)(2,1)} async-done(((bf16[96,768]{1,0:T(8,128)(2,1)}), bf16[768,768]{1,0:T(8,128)(2,1)}) %all-gather.8.cloned.1.call-update) | async-done | bytes 1179664 | tf_op jit(solution)/shard_map/all_gather | solution.py:190
  251.7 7.6 multiply_convert_fusion.3
  259.3 34.3 %all-gather.10.cloned.1.call-done = bf16[768,768]{0,1:T(8,128)(2,1)} async-done(((bf16[768,96]{0,1:T(8,128)(2,1)}), bf16[768,768]{0,1:T(8,128)(2,1)}) %all-gather.10.cloned.1.call-update) | async-done | bytes 1179664 | tf_op jit(solution)/shard_map/all_gather | solution.py:191
  293.6 3.6 add_convert_fusion.1
  300.1 5.0 multiply_convert_fusion.2
  311.4 3.3 convolution_convert_fusion.1
  316.6 60.2 %all-reduce.5.cloned.1.call-done = (f32[512,768]{1,0:T(8,128)}, f32[512,768]{1,0:T(8,128)}) async-done(((f32[512,768]{1,0:T(8,128)}, f32[512,768]{1,0:T(8,128)}), (f32[512,768]{1,0:T(8,128)}, f32[512,768]{1,0:T(8,128)})) %all-reduce.5.cloned.1.call-update) | async-done | bytes 3145744 | tf_op jit(solution)/shard_map/psum | solution.py:95
  376.8 4.6 multiply_reduce_fusion.3
  400.2 3.5 fusion.112
  407.0 61.1 %all-reduce.7.cloned.1.call-done = (bf16[512,768]{1,0:T(8,128)(2,1)}, bf16[512,768]{1,0:T(8,128)(2,1)}, bf16[512,768]{1,0:T(8,128)(2,1)}, bf16[512,768]{1,0:T(8,128)(2,1)}) async-done(((bf16[512,768]{1,0:T(8,128)(2,1)}, bf16[512,768]{1,0:T(8,128)(2,1)}, bf16[512,768]{1,0:T(8,128)(2,1)}, bf16[512,768]{1,0:T(8,128)(2,1)}), (bf16[512,768]{1,0:T(8,128)(2,1)}, bf16[512,768]{1,0:T(8,128)(2,1)}, ...) | async-done | bytes 3145744 | tf_op jit(solution)/shard_map/psum | solution.py:87
  468.1 2.5 fusion.9
  470.8 2.5 fusion.12
  474.5 4.4 convolution_add_fusion.1
  479.0 2.4 fusion.78
  481.4 2.3 convolution_add_fusion
  486.8 2.5 convolution_add_fusion.2
  489.4 44.6 %reduce-scatter.16.cloned.1.call-done = f32[96,192]{1,0:T(8,128)} async-done(((f32[768,192]{1,0:T(8,128)}), f32[96,192]{1,0:T(8,128)}) %reduce-scatter.16.cloned.1.call-update) | async-done | bytes 73744
  535.7 2.7 add_bitcast_fusion.1
  543.6 54.5 %reduce-scatter.18.cloned.1.call-done = f32[96,4]{1,0:T(8,128)} async-done(((f32[768,4]{1,0:T(8,128)}), f32[96,4]{1,0:T(8,128)}) %reduce-scatter.18.cloned.1.call-update) | async-done | bytes 1552
  600.2 69.8 %reduce-scatter.12.cloned.1.call-done = f32[96,768]{1,0:T(8,128)} async-done(((f32[768,768]{1,0:T(8,128)}), f32[96,768]{1,0:T(8,128)}) %reduce-scatter.12.cloned.1.call-update) | async-done | bytes 294928 | tf_op jit(solution)/shard_map/reduce_scatter | solution.py:200
  671.6 70.1 %reduce-scatter.14.cloned.1.call-done = f32[768,96]{0,1:T(8,128)} async-done(((f32[768,768]{0,1:T(8,128)}), f32[768,96]{0,1:T(8,128)}) %reduce-scatter.14.cloned.1.call-update) | async-done | bytes 294928 | tf_op jit(solution)/shard_map/reduce_scatter | solution.py:201
  743.3 70.2 %reduce-scatter.10.cloned.1.call-done = f32[96,3,192]{2,0,1:T(8,128)} async-done(((f32[768,3,192]{2,0,1:T(8,128)}), f32[96,3,192]{2,0,1:T(8,128)}) %reduce-scatter.10.cloned.1.call-update) | async-done | bytes 221200 | tf_op jit(solution)/shard_map/reduce_scatter | solution.py:198
  819.2 39.5 %psum.55 = f32[]{:T(128)} all-reduce(f32[]{:T(128)S(6)} %add.319), channel_id=1, replica_groups=mesh['dp'=8,'tp'=4] {'dp','tp'}, use_global_device_ids=true, to_apply=%region_53.54 | all-reduce | flops 1 | bytes 8 | tf_op jit(solution)/shard_map/psum | solution.py:216
  (404 shorter events, 86.7 us)
Async XLA Ops:
  7.2 152.1 %all-gather.14.cloned.1.call-start = ((), (), s32[]{:S(2)}) async-start(), calls=%async_computation.8 | async-start | bytes 7864320 | tf_op jit(solution)/shard_map/all_gather | solution.py:80
  10.0 61.7 %copy-start.80 = (f32[512]{0:T(512)}, f32[512]{0:T(512)S(1)}, u32[]{:S(2)}) copy-start(f32[512]{0:T(512)S(1)} %get-tuple-element.106) | copy-start | bytes 6148
  10.0 104.9 %copy-start.82 = (f32[512]{0:T(512)}, f32[512]{0:T(512)S(1)}, u32[]{:S(2)}) copy-start(f32[512]{0:T(512)S(1)} %get-tuple-element.107) | copy-start | bytes 6148
  11.2 60.5 %copy-start.101 = (f32[512]{0:T(512)}, f32[512]{0:T(512)S(1)}, u32[]{:S(2)}) copy-start(f32[512]{0:T(512)S(1)} %fusion.100) | copy-start | bytes 6148
  34.2 80.8 %copy-start.72 = (f32[768]{0:T(1024)}, f32[768]{0:T(1024)S(1)}, u32[]{:S(2)}) copy-start(f32[768]{0:T(1024)S(1)} %get-tuple-element.41) | copy-start | bytes 9220
  113.2 94.6 %all-gather.12.cloned.1.call-start = ((), (), s32[]{:S(2)}) async-start(), calls=%async_computation.7 | async-start | bytes 7864320 | tf_op jit(solution)/shard_map/all_gather | solution.py:80
  122.8 128.9 %all-gather.8.cloned.1.call-start = ((), (), s32[]{:S(2)}) async-start(), calls=%async_computation.5 | async-start | bytes 1327104 | tf_op jit(solution)/shard_map/all_gather | solution.py:190
  124.5 169.0 %all-gather.10.cloned.1.call-start = ((), (), s32[]{:S(2)}) async-start(), calls=%async_computation.6 | async-start | bytes 1327104 | tf_op jit(solution)/shard_map/all_gather | solution.py:191
  126.3 250.5 %all-reduce.5.cloned.1.call-start = ((), (), s32[]{:S(2)}) async-start(), calls=%async_computation.14 | async-start | bytes 6291456 | tf_op jit(solution)/shard_map/psum | solution.py:95
  309.2 158.9 %all-reduce.7.cloned.1.call-start = ((), (), s32[]{:S(2)}) async-start(), calls=%async_computation.15 | async-start | bytes 6291456 | tf_op jit(solution)/shard_map/psum | solution.py:87
  398.9 135.1 %reduce-scatter.16.cloned.1.call-start = ((), (), s32[]{:S(2)}) async-start(), calls=%async_computation.12 | async-start | bytes 884736
  405.5 62.6 %copy-start.3 = (bf16[2,512,768]{2,1,0:T(8,128)(2,1)S(1)}, bf16[2,512,768]{2,1,0:T(8,128)(2,1)}, u32[]{:S(2)}) copy-start(bf16[2,512,768]{2,1,0:T(8,128)(2,1)} %param.19) | copy-start | bytes 4718596
  405.5 62.6 %copy-start.73 = (f32[768]{0:T(1024)S(1)}, f32[768]{0:T(1024)}, u32[]{:S(2)}) copy-start(f32[768]{0:T(1024)} %copy-done.72) | copy-start | bytes 9220
  405.5 62.5 %copy-start.81 = (f32[512]{0:T(512)S(1)}, f32[512]{0:T(512)}, u32[]{:S(2)}) copy-start(f32[512]{0:T(512)} %copy-done.80) | copy-start | bytes 6148
  405.5 62.5 %copy-start.83 = (f32[512]{0:T(512)S(1)}, f32[512]{0:T(512)}, u32[]{:S(2)}) copy-start(f32[512]{0:T(512)} %copy-done.82) | copy-start | bytes 6148
  406.7 191.3 %reduce-scatter.18.cloned.1.call-start = ((), (), s32[]{:S(2)}) async-start(), calls=%async_computation.13 | async-start | bytes 442368
  474.4 195.5 %reduce-scatter.12.cloned.1.call-start = ((), (), s32[]{:S(2)}) async-start(), calls=%async_computation.10 | async-start | bytes 2654208 | tf_op jit(solution)/shard_map/reduce_scatter | solution.py:200
  478.9 262.8 %reduce-scatter.14.cloned.1.call-start = ((), (), s32[]{:S(2)}) async-start(), calls=%async_computation.11 | async-start | bytes 2654208 | tf_op jit(solution)/shard_map/reduce_scatter | solution.py:201
  483.7 329.9 %reduce-scatter.10.cloned.1.call-start = ((), (), s32[]{:S(2)}) async-start(), calls=%async_computation.9 | async-start | bytes 2654208 | tf_op jit(solution)/shard_map/reduce_scatter | solution.py:198
  489.3 46.3 %copy-start.128 = (f32[512]{0:T(512)S(1)}, f32[512]{0:T(512)}, u32[]{:S(2)}) copy-start(f32[512]{0:T(512)} %get-tuple-element.25) | copy-start | bytes 6148
  489.3 46.3 %copy-start.127 = (f32[512]{0:T(512)S(1)}, f32[512]{0:T(512)}, u32[]{:S(2)}) copy-start(f32[512]{0:T(512)} %get-tuple-element.26) | copy-start | bytes 6148
  489.3 46.3 %copy-start.84 = (f32[512]{0:T(512)S(1)}, f32[512]{0:T(512)}, u32[]{:S(2)}) copy-start(f32[512]{0:T(512)} %copy-done.82) | copy-start | bytes 6148
  489.3 46.3 %copy-start.100 = (f32[512]{0:T(512)S(1)}, f32[512]{0:T(512)}, u32[]{:S(2)}) copy-start(f32[512]{0:T(512)} %copy-done.99) | copy-start | bytes 6148
  489.3 46.3 %copy-start.107 = (f32[512]{0:T(512)S(1)}, f32[512]{0:T(512)}, u32[]{:S(2)}) copy-start(f32[512]{0:T(512)} %copy-done.105) | copy-start | bytes 6148
  489.3 46.3 %copy-start.111 = (f32[512]{0:T(512)S(1)}, f32[512]{0:T(512)}, u32[]{:S(2)}) copy-start(f32[512]{0:T(512)} %copy-done.110) | copy-start | bytes 6148
  817.9 43.0 %copy-start.34 = (f32[768,96]{0,1:T(8,128)S(1)}, f32[768,96]{0,1:T(8,128)}, u32[]{:S(2)}) copy-start(f32[768,96]{0,1:T(8,128)} %param.26) | copy-start | bytes 884740
  817.9 43.0 %copy-start.39 = (f32[768,96]{0,1:T(8,128)S(1)}, f32[768,96]{0,1:T(8,128)}, u32[]{:S(2)}) copy-start(f32[768,96]{0,1:T(8,128)} %reduce-scatter.14.cloned.1.call-done) | copy-start | bytes 884740
  817.9 43.0 %copy-start.57 = (f32[768,96]{0,1:T(8,128)S(1)}, f32[768,96]{0,1:T(8,128)}, u32[]{:S(2)}) copy-start(f32[768,96]{0,1:T(8,128)} %param.31) | copy-start | bytes 884740
  817.9 42.9 %copy-start.58 = (f32[768,96]{0,1:T(8,128)S(1)}, f32[768,96]{0,1:T(8,128)}, u32[]{:S(2)}) copy-start(f32[768,96]{0,1:T(8,128)} %param.36) | copy-start | bytes 884740
  819.2 42.8 %copy-start.38 = (f32[96,768]{1,0:T(8,128)S(1)}, f32[96,768]{1,0:T(8,128)}, u32[]{:S(2)}) copy-start(f32[96,768]{1,0:T(8,128)} %reduce-scatter.12.cloned.1.call-done) | copy-start | bytes 884740
  819.2 42.8 %copy-start.59 = (f32[96,768]{1,0:T(8,128)S(1)}, f32[96,768]{1,0:T(8,128)}, u32[]{:S(2)}) copy-start(f32[96,768]{1,0:T(8,128)} %param.30) | copy-start | bytes 884740
  819.2 42.8 %copy-start.60 = (f32[96,768]{1,0:T(8,128)S(1)}, f32[96,768]{1,0:T(8,128)}, u32[]{:S(2)}) copy-start(f32[96,768]{1,0:T(8,128)} %param.35) | copy-start | bytes 884740
  (119 other events, 666.3 us)
Sparse Core Ops, SparseCore 0:
  113.3 45.8 all-gather.13
  161.4 46.3 all-gather.11
  210.6 41.0 all-gather.7
  253.7 39.8 all-gather.9
  309.3 67.4 all-reduce.4
  398.9 69.0 all-reduce.6
  471.4 62.5 reduce-scatter.15
  537.6 60.3 reduce-scatter.17
  601.9 67.9 reduce-scatter.11
  673.7 67.9 reduce-scatter.13
  745.6 67.9 reduce-scatter.9
